TPU v7x, 32 devices: a whole 2x2x4 slice. The times are simulated.
32 devices in a mesh: term: 8 (over y, x, core), rep: 4 (over z).
Axes of the slice: x: 2, y: 2, z: 4, core: 2. Of those that a mesh axis runs over, the one named last changes fastest.
Arguments:
- panel_values: float32 [16, 8, 128, 128], P('rep', 'term'), may hold values from 0.01 to 0.3
- panel_ids: int32 [16, 8], P('rep', 'term'), may hold values from 0 to 1953, as said below
- block_rows: int32 [1792], P('term'), may hold values from 0 to 1953, as said below
- block_cols: int32 [1792], P('term'), may hold values from 0 to 1953, as said below
Outputs:
- blocks_out: float32 [1792, 128, 128], P(('term', 'rep'))
Inputs may be any that keep to these rules, and one draw needn't show every extreme that they name: `panel_ids`: the 8 tile ids of one panel are distinct. For every output block b, some panel lists both block_rows[b] and block_cols[b]. For every output block b, some panel lists both block_rows[b] and block_cols[b].
All inputs are finite; a program needn't handle non-finite values.
Results may differ from a plain program's by a relative error of at most 0.0003.
Values sent between devices are 32-bit elements; how exact they have to be, the bound alone decides.
A program may use at most 192 MiB of HBM per device.

v0:
```python
import jax
import jax.numpy as jnp
from jax import lax
from jax.sharding import PartitionSpec as P


def side_tiles(flat_values, tile_ids, wanted):
    match = tile_ids[:, None, :] == wanted[None, :, None]
    slots = jnp.argmax(match, axis=2)
    present = jnp.any(match, axis=2)
    offsets = (jnp.arange(tile_ids.shape[0], dtype=jnp.int32) * tile_ids.shape[1])[:, None]
    picked = jnp.take(flat_values, slots + offsets, axis=0)
    return jnp.where(present[:, :, None, None], picked, jnp.float32(0.0))


def all_terms(values_all, ids_all, block_rows, block_cols):
    panel_count, slot_count, passages, tile_size = values_all.shape
    flat_values = values_all.reshape(panel_count * slot_count, passages, tile_size)
    count = block_rows.shape[0]
    width = count // 4

    def one_group(pair):
        left_tile = side_tiles(flat_values, ids_all, pair[0])
        right_tile = side_tiles(flat_values, ids_all, pair[1])
        return jnp.einsum("qgpi,qgpj->gij", left_tile, right_tile, precision=lax.Precision.HIGHEST)

    grouped = lax.map(one_group, (block_rows.reshape(4, width), block_cols.reshape(4, width)))
    return grouped.reshape(count, tile_size, tile_size)


def local(panel_values, panel_ids, block_rows, block_cols):
    panel_count = panel_values.shape[0]
    value_list = []
    id_list = []
    for panel in range(panel_count):
        tile_values, tile_ids = (
            lax.all_gather(panel_values[panel], "term", axis=0, tiled=True),
            lax.all_gather(panel_ids[panel], "term", axis=0, tiled=True),
        )
        value_list.append(tile_values)
        id_list.append(tile_ids)
    values_all = jnp.stack(value_list)
    ids_all = jnp.stack(id_list)
    partial_value = all_terms(values_all, ids_all, block_rows, block_cols)
    return lax.psum_scatter(partial_value, "rep", scatter_dimension=0, tiled=True)


def solution(mesh):
    placed = (P("rep", "term", None, None), P("rep", "term"), P("term"), P("term"))
    return jax.shard_map(
        local, mesh=mesh, in_specs=placed, out_specs=P(("term", "rep"), None, None), check_vma=False
    )
```

profile of v0, /device:TPU:0, one launch (start us, length us, event | category | flops | bytes accessed | tf_op | source)
XLA Modules:
  0.0 594.3 jit_solution(17614716210860360679)
XLA Ops:
  8.9 11.3 %all-gather.4 = f32[8,1,128,128]{3,2,1,0:T(8,128)S(1)} all-gather(f32[1,1,128,128]{3,2,1,0:T(8,128)S(1)} %get-tuple-element.67), channel_id=6, replica_groups=mesh['term'=8,'rep'=4] {'term'}, dimensions={0}, use_global_device_ids=true | all-gather | bytes 589824 | tf_op jit(solution)/shard_map/all_gather | solution.py:37
  20.3 9.8 %all-gather.5 = f32[8,1,128,128]{3,2,1,0:T(8,128)S(1)} all-gather(f32[1,1,128,128]{3,2,1,0:T(8,128)S(1)} %get-tuple-element.68), channel_id=7, replica_groups=mesh['term'=8,'rep'=4] {'term'}, dimensions={0}, use_global_device_ids=true | all-gather | bytes 589824 | tf_op jit(solution)/shard_map/all_gather | solution.py:37
  30.1 9.9 %all-gather.6 = f32[8,1,128,128]{3,2,1,0:T(8,128)} all-gather(f32[1,1,128,128]{3,2,1,0:T(8,128)S(1)} %get-tuple-element.70), channel_id=8, replica_groups=mesh['term'=8,'rep'=4] {'term'}, dimensions={0}, use_global_device_ids=true | all-gather | bytes 589824 | tf_op jit(solution)/shard_map/all_gather | solution.py:37
  40.0 10.7 %all-gather.7 = f32[8,1,128,128]{3,2,1,0:T(8,128)} all-gather(f32[1,1,128,128]{3,2,1,0:T(8,128)S(1)} %get-tuple-element.69), channel_id=9, replica_groups=mesh['term'=8,'rep'=4] {'term'}, dimensions={0}, use_global_device_ids=true | all-gather | bytes 589824 | tf_op jit(solution)/shard_map/all_gather | solution.py:37
  59.0 7.0 %all-reduce.4 = (s32[8]{0:T(128)S(1)}, s32[8]{0:T(128)S(1)}, s32[8]{0:T(128)S(1)}, s32[8]{0:T(128)S(1)}) all-reduce(s32[8]{0:T(128)S(1)} %bitcast_dynamic-update-slice_fusion.1, s32[8]{0:T(128)S(1)} %bitcast_dynamic-update-slice_fusion.2, s32[8]{0:T(128)S(1)} %bitcast_dynamic-update-slice_fusion.3, ...), channel_id=5, replica_groups=mesh['term'=8,'rep'=4] {'term'}, use_global_device_ids=true, to_apply=%add.3 | all-reduce | flops 32 | bytes 256
  67.4 273.9 %while.10 = (s32[]{:T(128)}, f32[4,56,128,128]{3,2,1,0:T(8,128)}, s32[4,8]{1,0:T(4,128)S(1)}, s32[4,56]{1,0:T(4,128)S(1)}, f32[32,128,128]{2,1,0:T(8,128)S(1)}, /*index=5*/s32[4,56]{1,0:T(4,128)S(1)}, s32[]{:T(128)}) while((s32[]{:T(128)}, f32[4,56,128,128]{3,2,1,0:T(8,128)}, s32[4,8]{1,0:T(4,128)S(1)}, s32[4,56]{1,0:T(4,128)S(1)}, ...), condition=%wide.region_5.7_spmd, body=%wide.region_0.6_spmd.sunk | while | flops 5651862016 | bytes 150498224 | solution.py:27
  68.9 6.7 %gather_fusion = f32[224,128,128]{2,1,0:T(8,128)} fusion(f32[32,128,128]{2,1,0:T(8,128)S(1)} %get-tuple-element.150, s32[1024]{0:T(1024)S(1)} %pad_clamp_fusion.4), kind=kCustom, calls=%fused_computation.1.clone.clone.1 | custom fusion | bytes 29361024 | tf_op jit(solution)/shard_map/while/body/eval_jaxpr/jit(_take)/gather | solution.py:12
  75.6 15.3 %copy.41 = f32[4,56,128,128]{2,3,0,1:T(8,128)} copy(f32[4,56,128,128]{3,2,1,0:T(8,128)} %bitcast.38) | data formatting | bytes 29360128 | tf_op jit(solution)/shard_map/while/body/eval_jaxpr/jit(_take)/gather | solution.py:12
  97.6 15.3 %copy.44 = f32[4,56,128,128]{2,3,0,1:T(8,128)} copy(f32[4,56,128,128]{3,2,1,0:T(8,128)} %bitcast.39) | data formatting | bytes 29360128 | tf_op jit(solution)/shard_map/while/body/eval_jaxpr/jit(_take)/gather | solution.py:12
  113.5 22.3 %bitcast_dynamic-update-slice_fusion.6 = f32[4,56,128,128]{3,2,1,0:T(8,128)} fusion(f32[4,56,128,128]{3,2,1,0:T(8,128)} %get-tuple-element.140, s32[]{:T(128)} %get-tuple-element.139, f32[4,56,128,128]{2,3,0,1:T(8,128)} %copy.41, pred[4,56]{0,1:T(8,128)(4,1)S(1)} %copy.42, pred[4,56]{0,1:T(8,128)(4,1)S(1)} %copy.43, f32[4,56,128,128]{2,3,0,1:T(8,128)} %copy.44, ...), kind=kOutput, calls=%fused_computation.11.clone.1 | convolution fusion | flops 5651824640 | bytes 33031552 | tf_op jit(solution)/shard_map/while/body/eval_jaxpr/qgpi,qgpj->gij/dot_general | solution.py:25
  137.4 6.7 %gather_fusion = f32[224,128,128]{2,1,0:T(8,128)} fusion(f32[32,128,128]{2,1,0:T(8,128)S(1)} %get-tuple-element.150, s32[1024]{0:T(1024)S(1)} %pad_clamp_fusion.4), kind=kCustom, calls=%fused_computation.1.clone.clone.1 | custom fusion | bytes 29361024 | tf_op jit(solution)/shard_map/while/body/eval_jaxpr/jit(_take)/gather | solution.py:12
  144.1 15.3 %copy.41 = f32[4,56,128,128]{2,3,0,1:T(8,128)} copy(f32[4,56,128,128]{3,2,1,0:T(8,128)} %bitcast.38) | data formatting | bytes 29360128 | tf_op jit(solution)/shard_map/while/body/eval_jaxpr/jit(_take)/gather | solution.py:12
  159.4 6.6 %gather_fusion.1 = f32[224,128,128]{2,1,0:T(8,128)} fusion(f32[32,128,128]{2,1,0:T(8,128)S(1)} %get-tuple-element.150, s32[1024]{0:T(1024)S(1)} %pad_clamp_fusion.5), kind=kCustom, calls=%fused_computation.clone.clone.1 | custom fusion | bytes 29361024 | tf_op jit(solution)/shard_map/while/body/eval_jaxpr/jit(_take)/gather | solution.py:12
  166.0 15.3 %copy.44 = f32[4,56,128,128]{2,3,0,1:T(8,128)} copy(f32[4,56,128,128]{3,2,1,0:T(8,128)} %bitcast.39) | data formatting | bytes 29360128 | tf_op jit(solution)/shard_map/while/body/eval_jaxpr/jit(_take)/gather | solution.py:12
  181.9 22.4 %bitcast_dynamic-update-slice_fusion.6 = f32[4,56,128,128]{3,2,1,0:T(8,128)} fusion(f32[4,56,128,128]{3,2,1,0:T(8,128)} %get-tuple-element.140, s32[]{:T(128)} %get-tuple-element.139, f32[4,56,128,128]{2,3,0,1:T(8,128)} %copy.41, pred[4,56]{0,1:T(8,128)(4,1)S(1)} %copy.42, pred[4,56]{0,1:T(8,128)(4,1)S(1)} %copy.43, f32[4,56,128,128]{2,3,0,1:T(8,128)} %copy.44, ...), kind=kOutput, calls=%fused_computation.11.clone.1 | convolution fusion | flops 5651824640 | bytes 33031552 | tf_op jit(solution)/shard_map/while/body/eval_jaxpr/qgpi,qgpj->gij/dot_general | solution.py:25
  205.8 6.7 %gather_fusion = f32[224,128,128]{2,1,0:T(8,128)} fusion(f32[32,128,128]{2,1,0:T(8,128)S(1)} %get-tuple-element.150, s32[1024]{0:T(1024)S(1)} %pad_clamp_fusion.4), kind=kCustom, calls=%fused_computation.1.clone.clone.1 | custom fusion | bytes 29361024 | tf_op jit(solution)/shard_map/while/body/eval_jaxpr/jit(_take)/gather | solution.py:12
  212.6 15.3 %copy.41 = f32[4,56,128,128]{2,3,0,1:T(8,128)} copy(f32[4,56,128,128]{3,2,1,0:T(8,128)} %bitcast.38) | data formatting | bytes 29360128 | tf_op jit(solution)/shard_map/while/body/eval_jaxpr/jit(_take)/gather | solution.py:12
  234.5 15.3 %copy.44 = f32[4,56,128,128]{2,3,0,1:T(8,128)} copy(f32[4,56,128,128]{3,2,1,0:T(8,128)} %bitcast.39) | data formatting | bytes 29360128 | tf_op jit(solution)/shard_map/while/body/eval_jaxpr/jit(_take)/gather | solution.py:12
  250.4 22.4 %bitcast_dynamic-update-slice_fusion.6 = f32[4,56,128,128]{3,2,1,0:T(8,128)} fusion(f32[4,56,128,128]{3,2,1,0:T(8,128)} %get-tuple-element.140, s32[]{:T(128)} %get-tuple-element.139, f32[4,56,128,128]{2,3,0,1:T(8,128)} %copy.41, pred[4,56]{0,1:T(8,128)(4,1)S(1)} %copy.42, pred[4,56]{0,1:T(8,128)(4,1)S(1)} %copy.43, f32[4,56,128,128]{2,3,0,1:T(8,128)} %copy.44, ...), kind=kOutput, calls=%fused_computation.11.clone.1 | convolution fusion | flops 5651824640 | bytes 33031552 | tf_op jit(solution)/shard_map/while/body/eval_jaxpr/qgpi,qgpj->gij/dot_general | solution.py:25
  274.3 6.7 %gather_fusion = f32[224,128,128]{2,1,0:T(8,128)} fusion(f32[32,128,128]{2,1,0:T(8,128)S(1)} %get-tuple-element.150, s32[1024]{0:T(1024)S(1)} %pad_clamp_fusion.4), kind=kCustom, calls=%fused_computation.1.clone.clone.1 | custom fusion | bytes 29361024 | tf_op jit(solution)/shard_map/while/body/eval_jaxpr/jit(_take)/gather | solution.py:12
  281.0 15.3 %copy.41 = f32[4,56,128,128]{2,3,0,1:T(8,128)} copy(f32[4,56,128,128]{3,2,1,0:T(8,128)} %bitcast.38) | data formatting | bytes 29360128 | tf_op jit(solution)/shard_map/while/body/eval_jaxpr/jit(_take)/gather | solution.py:12
  303.0 15.3 %copy.44 = f32[4,56,128,128]{2,3,0,1:T(8,128)} copy(f32[4,56,128,128]{3,2,1,0:T(8,128)} %bitcast.39) | data formatting | bytes 29360128 | tf_op jit(solution)/shard_map/while/body/eval_jaxpr/jit(_take)/gather | solution.py:12
  318.9 22.4 %bitcast_dynamic-update-slice_fusion.6 = f32[4,56,128,128]{3,2,1,0:T(8,128)} fusion(f32[4,56,128,128]{3,2,1,0:T(8,128)} %get-tuple-element.140, s32[]{:T(128)} %get-tuple-element.139, f32[4,56,128,128]{2,3,0,1:T(8,128)} %copy.41, pred[4,56]{0,1:T(8,128)(4,1)S(1)} %copy.42, pred[4,56]{0,1:T(8,128)(4,1)S(1)} %copy.43, f32[4,56,128,128]{2,3,0,1:T(8,128)} %copy.44, ...), kind=kOutput, calls=%fused_computation.11.clone.1 | convolution fusion | flops 5651824640 | bytes 33031552 | tf_op jit(solution)/shard_map/while/body/eval_jaxpr/qgpi,qgpj->gij/dot_general | solution.py:25
  341.3 246.1 %reduce-scatter.2.cloned.1.call-done = f32[56,128,128]{2,1,0:T(8,128)} async-done(((f32[224,128,128]{2,1,0:T(8,128)}), f32[56,128,128]{2,1,0:T(8,128)}) %reduce-scatter.2.cloned.1.call-update) | async-done | bytes 3670032 | tf_op jit(solution)/shard_map/reduce_scatter | solution.py:45
  (77 shorter events, 40.3 us)
Async XLA Ops:
  6.5 580.9 %reduce-scatter.2.cloned.1.call-start = ((), (), s32[]{:S(2)}) async-start(), calls=%async_computation.1 | async-start | bytes 18350080 | tf_op jit(solution)/shard_map/reduce_scatter | solution.py:45
Sparse Core Ops, SparseCore 0:
  341.4 245.9 reduce-scatter.1
where the time goes:
time: 596 us; the launch traced here: 594 us
  waiting for transfers between devices  246 us (41%)
  local copies, waits for them, and re-layouts  189 us (32%)
  matrix products  89.5 us (15%)
  blocking collectives  48.8 us (8%)
  between operations  13.5 us (2%)
  other arithmetic  7.48 us (1%)
    reduce_scatter x1, waiting for transfers between devices, local(): lax.psum_scatter(partial_value, 'rep', scatter_dimension=0, tiled=True)  246 us
    gather x16, local copies, waits for them, and re-layouts, side_tiles(): picked = jnp.take(flat_values, slots + offsets, axis=0)  176 us
    dot_general x4, matrix products, one_group(): jnp.einsum('qgpi,qgpj->gij', left_tile, right_tile, precision=lax.Precisi...  89.5 us
    all_gather x4, blocking collectives, local(): lax.all_gather(panel_values[panel], 'term', axis=0, tiled=True)  41.8 us
  transfers between devices with their start and end apart: 1, of which 1 were waited for; matrix products, arithmetic and copies ran while one was open for 0% of the time, Pallas kernels for 0%

commit v1 on v0

v1 whole, which is shorter than its diff:
```python
import functools

import jax
import jax.numpy as jnp
from jax import lax
from jax.experimental import pallas as pl
from jax.experimental.pallas import tpu as pltpu
from jax.sharding import PartitionSpec as P

MESH = pl.DeviceIdType.MESH
CORES = 2
SIDE = 2
ID_ROWS = 8
UNROLL = 4


def gather_kernel(depth, shard_ref, all_ref, own_sem, send_sem, recv_sem):
    term = lax.axis_index("term")
    z = lax.axis_index("rep")
    core = term % CORES
    x = (term // CORES) % SIDE
    y = term // (CORES * SIDE)
    terms = CORES * SIDE * SIDE
    term_x = (y * SIDE + 1 - x) * CORES + core
    term_y = ((1 - y) * SIDE + x) * CORES + core
    term_c = (y * SIDE + x) * CORES + 1 - core
    UP, DOWN, X, Y, C = range(5)
    target = {UP: (term, z + 1), DOWN: (term, z - 1), X: (term_x, z), Y: (term_y, z), C: (term_c, z)}

    barrier = pltpu.get_barrier_semaphore()

    def greet(way):
        pl.semaphore_signal(barrier, inc=1, device_id=target[way], device_id_type=MESH)

    for way in (X, Y, C):
        greet(way)
    pl.when(z < depth - 1)(lambda: greet(UP))
    pl.when(z > 0)(lambda: greet(DOWN))
    pl.semaphore_wait(barrier, 3 + (z < depth - 1).astype(jnp.int32) + (z > 0).astype(jnp.int32))

    def slot_of(at_x, at_y, at_z, at_core):
        return at_z * terms + (at_y * SIDE + at_x) * CORES + at_core

    def copy(way, place, src=None):
        at_x, at_y, at_z = place
        slot = slot_of(at_x, at_y, at_z, core)
        return pltpu.make_async_remote_copy(
            src_ref=all_ref.at[slot] if src is None else src,
            dst_ref=all_ref.at[slot],
            send_sem=send_sem.at[way, (at_z * SIDE + at_y) * SIDE + at_x],
            recv_sem=recv_sem.at[slot],
            device_id=target[way],
            device_id_type=MESH,
        )

    sent = []

    def send(way, place, valid=None, src=None):
        sent.append((way, place, valid, src))
        if valid is None:
            copy(way, place, src).start()
        else:
            pl.when(valid)(lambda: copy(way, place, src).start())

    def arrived(at_x, at_y, at_z, at_core, valid=None):
        slot = slot_of(at_x, at_y, at_z, at_core)

        def take():
            pltpu.make_async_remote_copy(
                src_ref=all_ref.at[slot], dst_ref=all_ref.at[slot], send_sem=send_sem.at[0, 0],
                recv_sem=recv_sem.at[slot], device_id=target[C], device_id_type=MESH,
            ).wait_recv()

        if valid is None:
            take()
        else:
            pl.when(valid)(take)

    def both(a, b):
        return b if a is None else a if b is None else a & b

    def spread(at_z, valid, src=None):
        for way in (X, Y, C):
            send(way, (x, y, at_z), valid, src)

    def cross(at_z, valid):
        even = at_z % 2 == 0
        arrived(1 - x, y, at_z, core, valid)
        send(Y, (1 - x, y, at_z), both(valid, even))
        send(C, (1 - x, y, at_z), valid)
        arrived(x, 1 - y, at_z, core, valid)
        send(X, (x, 1 - y, at_z), both(valid, at_z % 2 == 1))
        send(C, (x, 1 - y, at_z), valid)

    def corner(at_z, valid):
        arrived(1 - x, 1 - y, at_z, core, valid)
        send(C, (1 - x, 1 - y, at_z), valid)

    own = pltpu.make_async_copy(shard_ref, all_ref.at[slot_of(x, y, z, core)], own_sem)
    own.start()
    send(UP, (x, y, z), z < depth - 1, shard_ref)
    send(DOWN, (x, y, z), z > 0, shard_ref)
    spread(z, None, shard_ref)

    def level(far):
        if far == 0:
            return [(z, None)]
        return [(z - far, z >= far), (z + far, z + far < depth)]

    for far in range(1, depth + 2):
        if far < depth:
            low, low_ok = level(far)[0]
            high, high_ok = level(far)[1]
            arrived(x, y, low, core, low_ok)
            send(UP, (x, y, low), low_ok & (z < depth - 1))
            spread(low, low_ok)
            arrived(x, y, high, core, high_ok)
            send(DOWN, (x, y, high), high_ok & (z > 0))
            spread(high, high_ok)
        if far - 1 < depth:
            for at_z, valid in level(far - 1):
                cross(at_z, valid)
        if far >= 2:
            for at_z, valid in level(far - 2):
                corner(at_z, valid)

    for at_z in range(depth):
        for at_y in range(SIDE):
            for at_x in range(SIDE):
                arrived(at_x, at_y, at_z, 1 - core)
    own.wait()
    for way, place, valid, src in sent:
        if valid is None:
            copy(way, place, src).wait_send()
        else:
            pl.when(valid)(lambda: copy(way, place, src).wait_send())


def gather_by_hand(shard, depth):
    terms = CORES * SIDE * SIDE
    return pl.pallas_call(
        functools.partial(gather_kernel, depth),
        out_shape=jax.ShapeDtypeStruct((depth * terms,) + shard.shape, shard.dtype),
        in_specs=[pl.BlockSpec(memory_space=pl.ANY)],
        out_specs=pl.BlockSpec(memory_space=pl.ANY),
        scratch_shapes=[
            pltpu.SemaphoreType.DMA,
            pltpu.SemaphoreType.DMA((5, depth * SIDE * SIDE)),
            pltpu.SemaphoreType.DMA((depth * terms,)),
        ],
        compiler_params=pltpu.CompilerParams(collective_id=0, has_side_effects=True),
    )(shard)


def product_kernel(slots, base, count_ref, list_ref, tiles_ref, out_ref, left_ref, right_ref):
    panel = pl.program_id(0)

    @pl.when(panel == 0)
    def _():
        def clear(b, _):
            out_ref[b] = jnp.zeros(out_ref.shape[1:], jnp.float32)
            return 0

        lax.fori_loop(0, out_ref.shape[0], clear, 0)

    size = tiles_ref.shape[-1]

    def split(value):
        high = value.astype(jnp.bfloat16)
        return high, (value - high.astype(jnp.float32)).astype(jnp.bfloat16)

    def prepare(s):
        value = tiles_ref[0, s]
        high, low = split(value)
        right_ref[s, :size] = high
        right_ref[s, size : 2 * size] = high
        right_ref[s, 2 * size :] = low
        high, low = split(value.T)
        left_ref[s, :, :size] = high
        left_ref[s, :, size : 2 * size] = low
        left_ref[s, :, 2 * size :] = high

    if slots <= 8:
        for s in range(slots):
            prepare(s)
    else:
        pl.loop(0, slots)(prepare)

    def entries(first, width):
        picked = []
        for k in range(width):
            code = list_ref[panel * base + first + k]
            pair = code % (slots * slots)
            picked.append((code // (slots * slots), pair // slots, pair % slots))
        sums = [
            out_ref[b] + jnp.dot(left_ref[r], right_ref[c], preferred_element_type=jnp.float32)
            for b, r, c in picked
        ]
        for (b, _, _), value in zip(picked, sums):
            out_ref[b] = value

    count = count_ref[panel]
    groups = count // UNROLL
    pl.loop(0, groups)(lambda i: entries(i * UNROLL, UNROLL))
    pl.loop(groups * UNROLL, count)(lambda i: entries(i, 1))


def products(tiles, slots, panels_each, counts, entries, blocks):
    groups, size = tiles.shape[0], tiles.shape[3]
    return pl.pallas_call(
        functools.partial(product_kernel, slots, entries.shape[1]),
        out_shape=jax.ShapeDtypeStruct((blocks, size, size), jnp.float32),
        grid_spec=pltpu.PrefetchScalarGridSpec(
            num_scalar_prefetch=2,
            grid=(groups * panels_each,),
            in_specs=[
                pl.BlockSpec(
                    (1, slots, size, size), lambda p, *_: (p // panels_each, 0, p % panels_each, 0)
                )
            ],
            out_specs=pl.BlockSpec((blocks, size, size), lambda p, *_: (0, 0, 0)),
            scratch_shapes=[
                pltpu.VMEM((slots, size, 3 * size), jnp.bfloat16),
                pltpu.VMEM((slots, 3 * size, size), jnp.bfloat16),
            ],
        ),
        compiler_params=pltpu.CompilerParams(
            dimension_semantics=("arbitrary",), vmem_limit_bytes=56 * 1024 * 1024
        ),
    )(counts, entries.reshape(-1), tiles)


def block_list(ids, rows, cols):
    slots, blocks = ids.shape[1], rows.shape[0]
    order = jnp.arange(slots, dtype=jnp.int32)[None, :, None]
    match_row = ids[:, :, None] == rows[None, None, :]
    match_col = ids[:, :, None] == cols[None, None, :]
    slot_row = jnp.sum(jnp.where(match_row, order, 0), axis=1)
    slot_col = jnp.sum(jnp.where(match_col, order, 0), axis=1)
    present = jnp.any(match_row, axis=1) & jnp.any(match_col, axis=1)
    number = jnp.arange(blocks, dtype=jnp.int32)
    code = (number[None, :] * slots + slot_row) * slots + slot_col
    ahead = jnp.sum(
        jnp.where(present[:, None, :] & (number[None, None, :] < number[None, :, None]), 1, 0), axis=2
    )
    chosen = present[:, None, :] & (ahead[:, None, :] == number[None, :, None])
    entries = jnp.sum(jnp.where(chosen, code[:, None, :], 0), axis=2)
    counts = jnp.sum(present.astype(jnp.int32), axis=1)
    return counts.astype(jnp.int32), entries.astype(jnp.int32)


def solution(mesh):
    depth, terms = mesh.shape["rep"], mesh.shape["term"]
    by_hand = terms == CORES * SIDE * SIDE

    def local(panel_values, panel_ids, block_rows, block_cols):
        panels_each, own_slots, passages, size = panel_values.shape
        blocks = block_rows.shape[0] // depth
        slots = terms * own_slots
        first = lax.axis_index("rep") * blocks
        rows = lax.dynamic_slice_in_dim(block_rows, first, blocks)
        cols = lax.dynamic_slice_in_dim(block_cols, first, blocks)
        if by_hand and own_slots == 1:
            ids = jnp.broadcast_to(panel_ids.reshape(-1).astype(jnp.float32)[:, None], (panels_each, size))
            ids = jnp.pad(ids, ((0, -panels_each % ID_ROWS), (0, 0)))
            shard = jnp.concatenate([panel_values.reshape(panels_each * passages, size), ids], axis=0)
            tiles = gather_by_hand(shard, depth).reshape(depth, terms, -1, size)
            start = panels_each * passages
            ids = tiles[:, :, start : start + panels_each, 0].astype(jnp.int32)
        else:
            shard = jnp.swapaxes(panel_values, 0, 1).reshape(own_slots, panels_each * passages, size)
            tiles = lax.all_gather(shard, ("rep", "term"), axis=0, tiled=True)
            tiles = tiles.reshape(depth, slots, panels_each * passages, size)
            ids = lax.all_gather(panel_ids.T, ("rep", "term"), axis=0, tiled=True)
            ids = ids.reshape(depth, slots, panels_each)
        ids = jnp.swapaxes(ids, 1, 2).reshape(depth * panels_each, slots)
        counts, entries = block_list(ids, rows, cols)
        return products(tiles, slots, panels_each, counts, entries, blocks)

    placed = (P("rep", "term", None, None), P("rep", "term"), P("term"), P("term"))
    return jax.shard_map(
        local, mesh=mesh, in_specs=placed, out_specs=P(("term", "rep"), None, None), check_vma=False
    )
```

time: 596 us -> 75.8 us (0.13)
  waiting for transfers between devices: 246 us -> 0 us
  local copies, waits for them, and re-layouts: 189 us -> 2.34 us
  matrix products: 89.5 us -> 0 us
  Pallas kernels: 0 us -> 67.6 us
  blocking collectives: 48.8 us -> 0 us
  between operations: 13.5 us -> 0.05 us
    reduce_scatter x1 -> x0, waiting for transfers between devices: 246 us -> none  [local(): lax.psum_scatter(partial_value, 'rep', scatter_dimension=0, tiled=True)]
    gather x16 -> x0, local copies, waits for them, and re-layouts: 176 us -> none  [side_tiles(): picked = jnp.take(flat_values, slots + offsets, axis=0)]
    dot_general x4 -> x0, matrix products: 89.5 us -> none  [one_group(): jnp.einsum('qgpi,qgpj->gij', left_tile, right_tile, precision=lax.Precisi...]
    pallas_call x0 -> x2, Pallas kernels: none -> 67.6 us  [the longest x1 46.1 us: gather_by_hand(): pl.pallas_call(functools.partial(gather_kernel, depth), out_shape=jax.Sha...]
    all_gather x4 -> x0, blocking collectives: 41.8 us -> none  [local(): lax.all_gather(panel_values[panel], 'term', axis=0, tiled=True)]
    unnamed x1 -> x0, blocking collectives: 7.03 us -> none
    another operation x10 -> x0, other arithmetic: 6.72 us -> none  [the longest x8 5.34 us: side_tiles(): slots = jnp.argmax(match, axis=2)]
    unnamed x9 -> x0, local copies, waits for them, and re-layouts: 6.64 us -> none
  transfers between devices with their start and end apart: 1 -> 0, of which waited for: 1 -> 0; matrix products, arithmetic and copies ran while one was open for 0% -> 0% of each run, Pallas kernels for 0% -> 0%
where the time goes in v1:
time: 75.8 us; the launch traced here: 75 us
  Pallas kernels  67.6 us (89%)
  other arithmetic  4.99 us (7%)
  local copies, waits for them, and re-layouts  2.34 us (3%)
    pallas_call x1, Pallas kernels, gather_by_hand(): pl.pallas_call(functools.partial(gather_kernel, depth), out_shape=jax.Sha...  46.1 us
    pallas_call x1, Pallas kernels, products(): pl.pallas_call(functools.partial(product_kernel, slots, entries.shape[1])...  21.6 us
    concatenate x2, other arithmetic, local(): jnp.concatenate([panel_values.reshape(panels_each * passages, size), ids]...  1.8 us

profile of v1, /device:TPU:0, one launch (start us, length us, event | category | flops | bytes accessed | tf_op | source)
XLA Modules:
  0.0 75.0 jit_solution(14388737635654819723)
XLA Ops:
  0.0 0.8 %dynamic_slice.6 = s32[56]{0:T(128)S(1)} dynamic-slice(s32[224]{0:T(256)} %param.6, s32[]{:T(128)S(6)} %select_n.19), dynamic_slice_sizes={56} | dynamic-slice | bytes 452 | tf_op jit(solution)/shard_map/dynamic_slice | solution.py:261
  0.8 0.8 %dynamic_slice.7 = s32[56]{0:T(128)S(1)} dynamic-slice(s32[224]{0:T(256)} %param.7, s32[]{:T(128)S(6)} %select_n.19), dynamic_slice_sizes={56} | dynamic-slice | bytes 452 | tf_op jit(solution)/shard_map/dynamic_slice | solution.py:262
  1.5 0.7 convert_bitcast_fusion
  2.2 1.8 %pad_maximum_fusion.shard_ref = f32[520,128]{1,0:T(8,128)} fusion(f32[512,128]{1,0:T(8,128)} %bitcast.11, f32[520]{0:T(1024)S(1)} %pad_select_fusion), kind=kLoop, calls=%fused_computation.4 | loop fusion | flops 66560 | bytes 530464 | tf_op jit(solution)/shard_map/concatenate | solution.py:266
  4.0 46.1 %shard_map.46 = f32[32,520,128]{2,1,0:T(8,128)} custom-call(f32[520,128]{1,0:T(8,128)} %pad_maximum_fusion.shard_ref), custom_call_target="tpu_custom_call" | custom-call | tf_op jit(solution)/shard_map/pallas_call | solution.py:141
  50.1 0.9 %slice_convert_fusion = s32[4,8,4,1]{3,2,1,0:T(4,128)S(1)} fusion(f32[4,8,520,128]{3,2,1,0:T(8,128)} %bitcast.9), kind=kLoop, calls=%fused_computation.11 | loop fusion | flops 128 | bytes 1024 | tf_op jit(solution)/shard_map/convert_element_type | solution.py:269
  51.0 0.2 copy.7
  51.1 0.1 compare_reduce_fusion
  51.3 0.1 fusion.1
  51.4 0.7 convert_reduce_fusion
  52.1 0.3 select_reduce_fusion.1
  52.4 0.4 select_reduce_fusion
  52.8 0.7 reshape.60.list_ref
  53.5 21.6 %shard_map.47 = f32[56,128,128]{2,1,0:T(8,128)} custom-call(s32[16]{0:T(128)} %get-tuple-element.9.count_ref, s32[896]{0:T(1024)} %reshape.60.list_ref, f32[4,8,520,128]{3,2,1,0:T(8,128)} %bitcast.10), custom_call_target="tpu_custom_call" | custom-call | tf_op jit(solution)/shard_map/pallas_call | solution.py:210
  (3 shorter events, 0.0 us)
